TPU v7x, 256 devices: a whole 4x4x8 slice. The times are simulated.
256 devices in a mesh: seq: 32 (over x, z), head: 8 (over y, core).
Axes of the slice: x: 4, y: 4, z: 8, core: 2. Of those that a mesh axis runs over, the one named last changes fastest.
Arguments:
- queries: bfloat16 [4096, 8192], P('seq', 'head'), may hold values from -250 to 250
- key_vectors: bfloat16 [4096, 1024], P('seq', 'head'), may hold values from -250 to 250
- value_vectors: bfloat16 [4096, 1024], P('seq', 'head'), may hold values from -20 to 20
- positions: int32 [4096], P('seq'), may hold values from 0 to 2047, as said below
- query_map: float32 [64, 128, 128], P('head'), may hold values from -0.5 to 0.5
- key_map: float32 [8, 128, 128], P('head'), may hold values from -0.5 to 0.5
Outputs:
- grad_queries: float32 [4096, 8192], P('seq', 'head')
- grad_keys: float32 [4096, 1024], P('seq', 'head')
- grad_values: float32 [4096, 1024], P('seq', 'head')
- query_map_grad: float32 [64, 128, 128], P('head')
- key_map_grad: float32 [8, 128, 128], P('head')
Inputs may be any that keep to these rules, and one draw needn't show every extreme that they name: positions[0] is 0, and each later position is either 0 (a document begins) or one more than the position before it; the slab holds at most 4 documents, and one of them is exactly 2048 tokens long.
All inputs are finite; a program needn't handle non-finite values.
Results may differ from a plain program's by a relative error of at most 0.0025.
Values may be sent and summed in bfloat16 or wider, within the bound.
No kernel may reach another device: no remote copies, remote signals or barrier semaphores. Data moves between devices by JAX's collectives and lax.ppermute only.
A program may use at most 64 MiB of HBM per device.

v0:
```python
import math
import jax
import jax.numpy as jnp
from jax import lax
from jax.sharding import PartitionSpec as P

HIGHEST = lax.Precision.HIGHEST
NEGATIVE = -1e30
epsilon = 1e-06


def entering(value, axis, join, neutral, backward):
    count, mine = (lax.axis_size(axis), lax.axis_index(axis))
    pieces = jax.tree.map(lambda part: lax.all_gather(part, axis), value)
    if backward:
        pieces = jax.tree.map(lambda part: part[::-1], pieces)
        mine = count - 1 - mine
    running = jax.tree.map(
        lambda part, zero: jnp.full_like(part, 0) + jnp.asarray(zero, part.dtype), value, neutral
    )

    def lap(position, running):
        longer = join(running, jax.tree.map(lambda part: part[position], pieces))
        return jax.tree.map(lambda new, old: jnp.where(position < mine, new, old), longer, running)

    return lax.fori_loop(0, count - 1, lap, running)


def feature_map(logits):
    return jnp.concatenate(
        [jax.nn.softmax(logits, axis=-1), jax.nn.softmax(-logits, axis=-1)], axis=-1
    )


def feature_back(phi, grad_phi, half_width):
    upper = phi[..., :half_width]
    lower = phi[..., half_width:]
    grad_up = grad_phi[..., :half_width]
    grad_low = grad_phi[..., half_width:]
    upper_part = upper * (grad_up - jnp.sum(upper * grad_up, axis=-1, keepdims=True))
    lower_part = lower * (grad_low - jnp.sum(lower * grad_low, axis=-1, keepdims=True))
    return upper_part - lower_part


def chain_states(earlier, later):
    carried = 1.0 - later[2]
    return (
        later[0] + carried * earlier[0],
        later[1] + carried * earlier[1],
        jnp.maximum(earlier[2], later[2]),
    )


def on_device(queries, key_vectors, value_vectors, positions, query_map, key_map):
    tok_rows = queries.shape[0]
    n_group = query_map.shape[0]
    head_dim = key_vectors.shape[1]
    half_width = query_map.shape[2]
    feat_width = 2 * half_width
    my_index = lax.axis_index("seq")
    row_base = my_index * tok_rows
    row_index = row_base + jnp.arange(tok_rows, dtype=jnp.int32)
    starts = row_index - positions
    last_start = starts[-1]
    q_heads = queries.reshape(tok_rows, n_group, head_dim)
    scaling = 1.0 / math.sqrt(head_dim)
    key_float = key_vectors.astype(jnp.float32)
    value_float = value_vectors.astype(jnp.float32)
    key_logits = jnp.dot(key_float, key_map[0], precision=HIGHEST)
    key_phi = feature_map(key_logits)
    initial = (
        jnp.full((n_group, tok_rows), NEGATIVE, jnp.float32),
        jnp.zeros((n_group, tok_rows), jnp.float32),
        jnp.zeros((n_group, tok_rows, head_dim), jnp.float32),
        jnp.zeros((feat_width, head_dim), jnp.float32),
        jnp.zeros((feat_width,), jnp.float32),
    )
    key_block = lax.all_gather(key_vectors, "seq", axis=0, tiled=True)
    value_block = lax.all_gather(value_vectors, "seq", axis=0, tiled=True)
    block_len = key_block.shape[0]
    key_index = jnp.arange(block_len, dtype=jnp.int32)
    visible = (key_index[None, :] <= row_index[:, None]) & (key_index[None, :] >= starts[:, None])

    def update(current):
        run_max, row_sum, summed, state_sum, norm_sums = current
        scores = (
            jnp.einsum("tgd,nd->gtn", q_heads, key_block, preferred_element_type=jnp.float32)
            * scaling
        )
        scores = jnp.where(visible[None], scores, NEGATIVE)
        new_max = jnp.maximum(run_max, jnp.max(scores, axis=-1))
        weights = jnp.where(visible[None], jnp.exp(scores - new_max[..., None]), 0.0)
        row_sum = jnp.sum(weights, axis=-1)
        summed = jnp.einsum(
            "gtn,nd->gtd",
            weights.astype(jnp.bfloat16),
            value_block,
            preferred_element_type=jnp.float32,
        )
        return (new_max, row_sum, summed, state_sum, norm_sums)

    run_max, row_sum, summed, state_sum, norm_sums = lax.cond(
        jnp.any(visible), update, lambda current: current, initial
    )
    held_teacher = jnp.transpose(summed / row_sum[..., None], (1, 0, 2))
    query_float = q_heads.astype(jnp.float32)
    query_logits = jnp.einsum("tgd,gdf->tgf", query_float, query_map, precision=HIGHEST)
    query_phi = feature_map(query_logits)
    visible_rows = (
        (row_index[None, :] <= row_index[:, None]) & (row_index[None, :] >= starts[:, None])
    ).astype(jnp.float32)
    crossing = (starts < row_base).astype(jnp.float32)
    keeping = (starts == last_start).astype(jnp.float32)
    fresh_doc = (last_start >= row_base).astype(jnp.float32).reshape(1)
    kept_phi = key_phi * keeping[:, None]
    state_local = jnp.dot(kept_phi.T, value_float, precision=HIGHEST)
    norms_local = jnp.sum(kept_phi, axis=0)
    state_in, norms_in, unused = entering(
        (state_local, norms_local, fresh_doc),
        "seq",
        chain_states,
        (jnp.zeros_like(state_local), jnp.zeros_like(norms_local), jnp.zeros((1,), jnp.float32)),
        False,
    )
    inner = jnp.einsum("tgf,jf->gtj", query_phi, key_phi, precision=HIGHEST) * visible_rows[None]
    numer = jnp.einsum("gtj,jd->tgd", inner, value_float, precision=HIGHEST)
    numer = numer + crossing[:, None, None] * jnp.einsum(
        "tgf,fd->tgd", query_phi, state_in, precision=HIGHEST
    )
    denom = jnp.sum(inner, axis=-1).T + crossing[:, None] * jnp.einsum(
        "tgf,f->tg", query_phi, norms_in, precision=HIGHEST
    )
    outputs = numer / denom[..., None]
    error = outputs - held_teacher
    grad_numer = error / denom[..., None]
    grad_denom = -jnp.sum(error * outputs, axis=-1) / denom
    mixing = (
        jnp.einsum("tgd,jd->gtj", grad_numer, value_float, precision=HIGHEST)
        + grad_denom.T[:, :, None]
    ) * visible_rows[None]
    grad_qphi = jnp.einsum("gtj,jf->tgf", mixing, key_phi, precision=HIGHEST)
    grad_qphi = grad_qphi + crossing[:, None, None] * (
        jnp.einsum("tgd,fd->tgf", grad_numer, state_in, precision=HIGHEST)
        + grad_denom[..., None] * norms_in
    )
    crossing_phi = query_phi * crossing[:, None, None]
    back_local = jnp.einsum("tgf,tgd->fd", crossing_phi, grad_numer, precision=HIGHEST)
    back_norms = jnp.einsum("tgf,tg->f", crossing_phi, grad_denom, precision=HIGHEST)
    back_in, back_norms_in, unused_flag = entering(
        (back_local, back_norms, fresh_doc),
        "seq",
        chain_states,
        (jnp.zeros_like(back_local), jnp.zeros_like(back_norms), jnp.zeros((1,), jnp.float32)),
        True,
    )
    grad_kphi = jnp.einsum("gtj,tgf->jf", mixing, query_phi, precision=HIGHEST)
    grad_kphi = grad_kphi + keeping[:, None] * (
        jnp.dot(value_float, back_in.T, precision=HIGHEST) + back_norms_in[None, :]
    )
    grad_values = jnp.einsum("gtj,tgd->jd", inner, grad_numer, precision=HIGHEST)
    grad_values = grad_values + keeping[:, None] * jnp.dot(key_phi, back_in, precision=HIGHEST)
    query_dlogit = feature_back(query_phi, grad_qphi, half_width)
    key_dlogit = feature_back(key_phi, grad_kphi, half_width)
    grad_queries = jnp.einsum("tgf,gdf->tgd", query_dlogit, query_map, precision=HIGHEST).reshape(
        tok_rows, n_group * head_dim
    )
    grad_keys = jnp.dot(key_dlogit, key_map[0].T, precision=HIGHEST)
    local_qmap = jnp.einsum("tgd,tgf->gdf", query_float, query_dlogit, precision=HIGHEST)
    local_kmap = jnp.dot(key_float.T, key_dlogit, precision=HIGHEST)[None]
    clip_limit = 0.25 * math.sqrt((n_group + 1) * lax.axis_size("head") * head_dim * half_width)
    summed_qmap, summed_kmap = lax.psum((local_qmap, local_kmap), "seq")
    squared = lax.psum(
        jnp.sum(summed_qmap * summed_qmap) + jnp.sum(summed_kmap * summed_kmap), "head"
    )
    factor = jnp.minimum(1.0, clip_limit / (jnp.sqrt(squared) + epsilon))
    query_map_grad = factor * summed_qmap
    key_map_grad = factor * summed_kmap
    return (grad_queries, grad_keys, grad_values, query_map_grad, key_map_grad)


def solution(mesh):
    placed = (
        P("seq", "head"),
        P("seq", "head"),
        P("seq", "head"),
        P("seq"),
        P("head", None, None),
        P("head", None, None),
    )
    return jax.shard_map(
        on_device,
        mesh=mesh,
        in_specs=placed,
        out_specs=(
            P("seq", "head"),
            P("seq", "head"),
            P("seq", "head"),
            P("head", None, None),
            P("head", None, None),
        ),
        check_vma=False,
    )
```

profile of v0, /device:TPU:1, one launch (start us, length us, event | category | flops | bytes accessed | tf_op | source)
XLA Modules:
  0.0 715.1 jit_solution(13117342215060472636)
XLA Ops:
  11.8 1.6 fusion.41
  14.3 39.5 %all-gather.4 = f32[32,1,256]{2,1,0:T(1,128)S(1)} all-gather(f32[1,1,256]{2,1,0:T(1,128)S(1)} %bitcast.184), channel_id=3, replica_groups=mesh['seq'=32,'head'=8] {'seq'}, dimensions={0}, use_global_device_ids=true | all-gather | bytes 33792 | tf_op jit(solution)/shard_map/all_gather | solution.py:14
  53.8 1.8 copy.60
  59.4 57.9 %all-reduce = f32[32]{0:T(128)S(1)} all-reduce(f32[32]{0:T(128)S(1)} %dynamic-update-slice), channel_id=1, replica_groups=mesh['seq'=32,'head'=8] {'seq'}, use_global_device_ids=true, to_apply=%add | all-reduce | flops 32 | bytes 256
  120.7 2.0 convolution_bitcast_fusion.3
  122.7 39.8 %all-gather.13.cloned.1.call-done = bf16[4096,128]{1,0:T(8,128)(2,1)} async-done(((bf16[128,128]{1,0:T(8,128)(2,1)}), bf16[4096,128]{1,0:T(8,128)(2,1)}) %all-gather.13.cloned.1.call-update) | async-done | bytes 1048592 | tf_op jit(solution)/shard_map/all_gather | solution.py:79
  162.5 12.8 %conditional.1 = (f32[8,128]{1,0:T(8,128)S(1)}, f32[8,128,128]{1,2,0:T(8,128)}) conditional(s32[]{:T(128)} %convert_element_type.26, () %tuple.45, (pred[128,4096]{0,1:T(8,128)(4,1)S(1)}, bf16[4096,128]{1,0:T(8,128)(2,1)}, bf16[128,8,128]{0,2,1:T(8,128)(2,1)}, bf16[4096,128]{1,0:T(8,128)(2,1)}) %tuple.46), branch_computations={%region_13.14_spmd, %region_14.17_spmd} | conditional | flops 2202008576 | bytes 59007020 | solution.py:102
  162.5 3.8 fusion
  166.4 4.8 fusion.3
  171.2 4.0 fusion.2
  175.4 70.9 %all-gather.15.cloned.1.call-done = f32[8192,128]{1,0:T(8,128)} async-done(((f32[256,128]{1,0:T(8,128)}), f32[8192,128]{1,0:T(8,128)}) %all-gather.15.cloned.1.call-update) | async-done | bytes 4194320 | tf_op jit(solution)/shard_map/all_gather | solution.py:14
  246.3 90.0 %while.32 = (s32[]{:T(128)}, f32[256,128]{1,0:T(8,128)S(1)}, f32[256]{0:T(256)S(1)}, s32[]{:T(128)}, f32[32,256,128]{2,1,0:T(8,128)}, /*index=5*/f32[32,1]{0,1:T...) while((s32[]{:T(128)}, f32[256,128]{1,0:T(8,128)S(1)}, f32[256]{0:T(256)S(1)}, s32[]{:T(128)}, ...), condition=%wide.region_10.11_spmd.clone, body=%wide.region_9.10_spmd.clone.sunk | while | flops 132101 | bytes 398487 | solution.py:26
  247.6 1.6 fusion.106
  250.5 1.6 fusion.106
  253.4 1.6 fusion.106
  256.3 1.6 fusion.106
  259.2 1.6 fusion.106
  262.1 1.6 fusion.106
  265.0 1.6 fusion.106
  267.9 1.6 fusion.106
  270.8 1.6 fusion.106
  273.7 1.6 fusion.106
  276.6 1.6 fusion.106
  279.5 1.6 fusion.106
  282.4 1.6 fusion.106
  285.3 1.6 fusion.106
  288.2 1.6 fusion.106
  291.1 1.6 fusion.106
  294.0 1.6 fusion.106
  296.9 1.6 fusion.106
  299.8 1.6 fusion.106
  302.7 1.6 fusion.106
  305.6 1.6 fusion.106
  308.5 1.6 fusion.106
  311.4 1.6 fusion.106
  314.3 1.6 fusion.106
  317.2 1.6 fusion.106
  320.1 1.6 fusion.106
  323.1 1.6 fusion.106
  326.0 1.6 fusion.106
  328.9 1.6 fusion.106
  331.8 1.6 fusion.106
  334.7 1.6 fusion.106
  337.0 2.1 multiply_reduce_fusion.3
  339.0 1.7 convolution_bitcast_fusion.6
  341.8 32.8 %all-gather.5 = f32[32,1,256]{2,1,0:T(1,128)S(1)} all-gather(f32[1,1,256]{2,1,0:T(1,128)S(1)} %convolution_bitcast_fusion.10), channel_id=5, replica_groups=mesh['seq'=32,'head'=8] {'seq'}, dimensions={0}, use_global_device_ids=true | all-gather | bytes 33792 | tf_op jit(solution)/shard_map/all_gather | solution.py:14
  375.7 1.6 convolution_bitcast_fusion.7
  379.7 2.4 convolution_bitcast_fusion.1
  382.1 37.8 %all-gather.17.cloned.1.call-done = f32[8192,128]{1,0:T(8,128)} async-done(((f32[256,128]{1,0:T(8,128)}), f32[8192,128]{1,0:T(8,128)}) %all-gather.17.cloned.1.call-update) | async-done | bytes 4194320 | tf_op jit(solution)/shard_map/all_gather | solution.py:14
  419.9 4.6 rev.9
  424.5 109.9 %while.33 = (s32[]{:T(128)}, f32[256,128]{1,0:T(8,128)S(1)}, f32[256]{0:T(256)S(1)}, s32[]{:T(128)}, f32[32,256,128]{2,1,0:T(8,128)}, /*index=5*/f32[32,1]{0,1:T(1,128)S(1)}, f32[32,256]{1,0:T(8,128)}, s32[]{:T(128)}, s32[]{:T(128)}) while((s32[]{:T(128)}, f32[256,128]{1,0:T(8,128)S(1)}, f32[256]{0:T(256)S(1)}, s32[]{:T(128)}, ...), condition=%wide.region_21.22_spmd.clone, body=%wide.region_20.21_spmd.clone.sunk | while | flops 132101 | bytes 398487 | solution.py:26
  429.9 1.6 fusion.108
  437.0 1.6 fusion.108
  444.1 1.6 fusion.108
  451.2 1.6 fusion.108
  458.3 1.6 fusion.108
  465.4 1.6 fusion.108
  483.1 1.6 fusion.108
  490.2 1.6 fusion.108
  497.3 1.6 fusion.108
  540.4 139.9 %all-reduce.4.cloned.1.call-done = (f32[8,128,128]{1,2,0:T(8,128)}, f32[1,128,128]{1,2,0:T(8,128)}) async-done(((f32[8,128,128]{1,2,0:T(8,128)}, f32[1,128,128]{1,2,0:T(8,128)}), (f32[8,128,128]{1,2,0:T(8,128)}, f32[1,128,128]{1,2,0:T(8,128)})) %all-reduce.4.cloned.1.call-update) | async-done | bytes 589840 | tf_op jit(solution)/shard_map/psum | solution.py:171
  681.7 1.8 multiply_reduce_fusion
  684.8 1.8 fusion.44
  686.6 17.6 %psum.23 = f32[]{:T(128)} all-reduce(f32[]{:T(128)S(6)} %add.151), channel_id=1, replica_groups=mesh['seq'=32,'head'=8] {'head'}, use_global_device_ids=true, to_apply=%region_28.29 | all-reduce | flops 1 | bytes 8 | tf_op jit(solution)/shard_map/psum | solution.py:172
  (275 shorter events, 161.0 us)
Async XLA Ops:
  7.2 110.2 %copy-start = (f32[8,128,128]{2,1,0:T(8,128)S(1)}, f32[8,128,128]{2,1,0:T(8,128)}, u32[]{:S(2)}) copy-start(f32[8,128,128]{2,1,0:T(8,128)} %param.16) | copy-start | bytes 1572868
  7.2 115.5 %all-gather.11.cloned.1.call-start = ((), (), s32[]{:S(2)}) async-start(), calls=%async_computation | async-start | bytes 1081344 | tf_op jit(solution)/shard_map/all_gather | solution.py:78
  7.9 154.6 %all-gather.13.cloned.1.call-start = ((), (), s32[]{:S(2)}) async-start(), calls=%async_computation.1 | async-start | bytes 1081344 | tf_op jit(solution)/shard_map/all_gather | solution.py:79
  8.7 237.7 %all-gather.15.cloned.1.call-start = ((), (), s32[]{:S(2)}) async-start(), calls=%async_computation.2 | async-start | bytes 4325376 | tf_op jit(solution)/shard_map/all_gather | solution.py:14
  13.5 406.4 %all-gather.17.cloned.1.call-start = ((), (), s32[]{:S(2)}) async-start(), calls=%async_computation.3 | async-start | bytes 4325376 | tf_op jit(solution)/shard_map/all_gather | solution.py:14
  162.5 212.7 %copy-start.1 = (bf16[128,128]{1,0:T(8,128)(2,1)S(1)}, bf16[128,128]{1,0:T(8,128)(2,1)}, u32[]{:S(2)}) copy-start(bf16[128,128]{1,0:T(8,128)(2,1)} %param.14) | copy-start | bytes 98308
  162.5 3.8 copy-start.2
  340.7 339.6 %all-reduce.4.cloned.1.call-start = ((), (), s32[]{:S(2)}) async-start(), calls=%async_computation.4 | async-start | bytes 1179648 | tf_op jit(solution)/shard_map/psum | solution.py:171
Sparse Core Ops, SparseCore 0:
  10.6 75.4 all-gather.10
  88.7 73.7 all-gather.12
  165.1 81.1 all-gather.14
  340.8 79.0 all-gather.16
  537.3 142.9 all-reduce.3
where the time goes:
time: 720 us; the launch traced here: 715 us
  waiting for transfers between devices  290 us (40%)
  other arithmetic  190 us (26%)
  blocking collectives  148 us (21%)
  local copies, waits for them, and re-layouts  34.3 us (5%)
  matrix products  34.1 us (5%)
  between operations  17.4 us (2%)
    psum x1, waiting for transfers between devices, on_device(): summed_qmap, summed_kmap = lax.psum((local_qmap, local_kmap), 'seq')  140 us
    select_n x124, other arithmetic, lap(): jnp.where(position < mine, new, old)  140 us
    all_gather x2, waiting for transfers between devices, entering(): pieces = jax.tree.map(lambda part: lax.all_gather(part, axis), value)  109 us
    all_gather x2, blocking collectives, entering(): pieces = jax.tree.map(lambda part: lax.all_gather(part, axis), value)  72.3 us
    unnamed x1, blocking collectives  57.9 us
    all_gather x1, waiting for transfers between devices, on_device(): value_block = lax.all_gather(value_vectors, 'seq', axis=0, tiled=True)  39.8 us
    sub x62, other arithmetic, chain_states(): carried = 1.0 - later[2]  36.6 us
    dynamic_slice x62, local copies, waits for them, and re-layouts, lap(): longer = join(running, jax.tree.map(lambda part: part[position], pieces))  21.9 us
  transfers between devices with their start and end apart: 5, of which 4 were waited for; matrix products, arithmetic and copies ran while one was open for 6% of the time, Pallas kernels for 0%

commit v1 on v0

--- a/solution.py
+++ b/solution.py
@@ -1,12 +1,23 @@
+import functools
 import math
 import jax
 import jax.numpy as jnp
 from jax import lax
 from jax.sharding import PartitionSpec as P
+from jax.lax import all_to_all, psum
 
 HIGHEST = lax.Precision.HIGHEST
 NEGATIVE = -1e30
 epsilon = 1e-06
+
+
+def deliver_object_now(slab_in, a_name, dim_no):
+    return jnp.concatenate(
+        all_to_all(jnp.stack([slab_in for _ in range(psum(1, a_name))]), a_name, 0, 0), dim_no
+    )
+
+
+report_pages = functools.partial(deliver_object_now, a_name="seq", dim_no=0)
 
 
 def entering(value, axis, join, neutral, backward):
@@ -76,7 +87,7 @@
         jnp.zeros((feat_width,), jnp.float32),
     )
     key_block = lax.all_gather(key_vectors, "seq", axis=0, tiled=True)
-    value_block = lax.all_gather(value_vectors, "seq", axis=0, tiled=True)
+    value_block = report_pages(value_vectors)
     block_len = key_block.shape[0]
     key_index = jnp.arange(block_len, dtype=jnp.int32)
     visible = (key_index[None, :] <= row_index[:, None]) & (key_index[None, :] >= starts[:, None])

time: 720 us -> 649 us (0.901)
  waiting for transfers between devices: 290 us -> 195 us
  starting transfers between devices: 0.2 us -> 12.2 us
  blocking collectives: 148 us -> 156 us
    all_gather x2, waiting for transfers between devices: 109 us -> 55 us  [entering(): pieces = jax.tree.map(lambda part: lax.all_gather(part, axis), value)]
    all_gather x1 -> x0, waiting for transfers between devices: 39.8 us -> none  [on_device(): value_block = lax.all_gather(value_vectors, 'seq', axis=0, tiled=True)]
    all_to_all x0 -> x1, starting transfers between devices: none -> 12 us  [deliver_object_now(): all_to_all(jnp.stack([slab_in for _ in range(psum(1, a_name))]), a_name,...]
    all_gather x2, blocking collectives: 72.3 us -> 80.3 us  [entering(): pieces = jax.tree.map(lambda part: lax.all_gather(part, axis), value)]
  transfers between devices with their start and end apart: 5 -> 5, of which waited for: 4 -> 3; matrix products, arithmetic and copies ran while one was open for 6% -> 7% of each run, Pallas kernels for 0% -> 0%
where the time goes in v1:
time: 649 us; the launch traced here: 644 us
  waiting for transfers between devices  195 us (30%)
  other arithmetic  190 us (29%)
  blocking collectives  156 us (24%)
  local copies, waits for them, and re-layouts  36.8 us (6%)
  matrix products  35.2 us (5%)
  between operations  17.4 us (3%)
  starting transfers between devices  12.2 us (2%)
    select_n x124, other arithmetic, lap(): jnp.where(position < mine, new, old)  140 us
    psum x1, waiting for transfers between devices, on_device(): summed_qmap, summed_kmap = lax.psum((local_qmap, local_kmap), 'seq')  140 us
    all_gather x2, blocking collectives, entering(): pieces = jax.tree.map(lambda part: lax.all_gather(part, axis), value)  80.3 us
    unnamed x1, blocking collectives  58.5 us
    all_gather x2, waiting for transfers between devices, entering(): pieces = jax.tree.map(lambda part: lax.all_gather(part, axis), value)  55 us
    sub x62, other arithmetic, chain_states(): carried = 1.0 - later[2]  36.6 us
    dynamic_slice x62, local copies, waits for them, and re-layouts, lap(): longer = join(running, jax.tree.map(lambda part: part[position], pieces))  22.3 us
    psum x1, blocking collectives, on_device(): lax.psum(jnp.sum(summed_qmap * summed_qmap) + jnp.sum(summed_kmap * summe...  17.6 us
  transfers between devices with their start and end apart: 5, of which 3 were waited for; matrix products, arithmetic and copies ran while one was open for 7% of the time, Pallas kernels for 0%

profile of v1, /device:TPU:1, one launch (start us, length us, event | category | flops | bytes accessed | tf_op | source)
XLA Modules:
  0.0 644.3 jit_solution(7642527102291334190)
XLA Ops:
  11.1 1.6 fusion.40
  12.7 2.0 stack.2
  14.7 12.0 %all-to-all-start = ((bf16[32,128,128]{2,1,0:T(8,128)(2,1)}), bf16[32,128,128]{2,1,0:T(8,128)(2,1)}, u32[]{:S(2)}, u32[]{:S(2)}) async-start(bf16[32,128,128]{2,1,0:T(8,128)(2,1)} %stack.2), calls=%async_computation | async-start | bytes 2097152 | tf_op jit(solution)/shard_map/all_to_all | solution.py:16
  27.4 1.8 copy.60
  31.2 48.5 %all-gather.4 = f32[32,1,256]{2,1,0:T(1,128)S(1)} all-gather(f32[1,1,256]{2,1,0:T(1,128)S(1)} %bitcast.185), channel_id=3, replica_groups=mesh['seq'=32,'head'=8] {'seq'}, dimensions={0}, use_global_device_ids=true | all-gather | bytes 33792 | tf_op jit(solution)/shard_map/all_gather | solution.py:25
  81.7 58.5 %all-reduce = f32[32]{0:T(128)S(1)} all-reduce(f32[32]{0:T(128)S(1)} %dynamic-update-slice), channel_id=1, replica_groups=mesh['seq'=32,'head'=8] {'seq'}, use_global_device_ids=true, to_apply=%add | all-reduce | flops 32 | bytes 256
  143.6 2.0 convolution_bitcast_fusion.3
  145.6 13.8 %conditional.1 = (f32[8,128]{1,0:T(8,128)S(1)}, f32[8,128,128]{1,2,0:T(8,128)}) conditional(s32[]{:T(128)} %convert_element_type.26, () %tuple.45, (pred[128,4096]{0,1:T(8,128)(4,1)S(1)}, bf16[4096,128]{1,0:T(8,128)(2,1)}, bf16[128,8,128]{0,2,1:T(8,128)(2,1)}, bf16[32,128,128]{2,1,0:T(8,128)(2,1)}) %tuple.46), branch_computations={%region_13.14_spmd, %region_14.17_spmd} | conditional | flops 2202008576 | bytes 54812688 | solution.py:113
  145.6 3.8 fusion
  149.4 4.0 fusion.2
  153.4 6.0 fusion.3
  159.4 13.3 %all-gather.12.cloned.1.call-done = f32[8192,128]{1,0:T(8,128)} async-done(((f32[256,128]{1,0:T(8,128)}), f32[8192,128]{1,0:T(8,128)}) %all-gather.12.cloned.1.call-update) | async-done | bytes 4194320 | tf_op jit(solution)/shard_map/all_gather | solution.py:25
  172.7 90.2 %while.32 = (s32[]{:T(128)}, f32[256,128]{1,0:T(8,128)S(1)}, f32[256]{0:T(256)S(1)}, s32[]{:T(128)}, f32[32,256,128]{2,1,0:T(8,128)}, /*index=5*/f32[32,1]{0,1:T...) while((s32[]{:T(128)}, f32[256,128]{1,0:T(8,128)S(1)}, f32[256]{0:T(256)S(1)}, s32[]{:T(128)}, ...), condition=%wide.region_10.11_spmd.clone, body=%wide.region_9.10_spmd.clone.sunk | while | flops 132101 | bytes 398487 | solution.py:37
  173.3 1.6 fusion.106
  176.2 1.6 fusion.106
  179.1 1.6 fusion.106
  182.0 1.6 fusion.106
  184.9 1.6 fusion.106
  187.8 1.6 fusion.106
  190.8 1.6 fusion.106
  193.7 1.6 fusion.106
  196.6 1.6 fusion.106
  199.5 1.6 fusion.106
  202.4 1.6 fusion.106
  205.3 1.6 fusion.106
  208.2 1.6 fusion.106
  211.1 1.6 fusion.106
  214.0 1.6 fusion.106
  216.9 1.6 fusion.106
  219.8 1.6 fusion.106
  222.8 1.6 fusion.106
  225.7 1.6 fusion.106
  228.6 1.6 fusion.106
  231.5 1.6 fusion.106
  234.4 1.6 fusion.106
  237.3 1.6 fusion.106
  240.2 1.6 fusion.106
  243.1 1.6 fusion.106
  246.0 1.6 fusion.106
  248.9 1.6 fusion.106
  251.8 1.6 fusion.106
  254.8 1.6 fusion.106
  257.7 1.6 fusion.106
  260.6 1.6 fusion.106
  263.5 2.1 multiply_reduce_fusion.3
  265.6 1.6 convolution_bitcast_fusion.6
  268.4 31.8 %all-gather.5 = f32[32,1,256]{2,1,0:T(1,128)S(1)} all-gather(f32[1,1,256]{2,1,0:T(1,128)S(1)} %convolution_bitcast_fusion.10), channel_id=5, replica_groups=mesh['seq'=32,'head'=8] {'seq'}, dimensions={0}, use_global_device_ids=true | all-gather | bytes 33792 | tf_op jit(solution)/shard_map/all_gather | solution.py:25
  301.2 1.6 convolution_bitcast_fusion.7
  305.2 2.4 convolution_bitcast_fusion.1
  307.6 41.7 %all-gather.14.cloned.1.call-done = f32[8192,128]{1,0:T(8,128)} async-done(((f32[256,128]{1,0:T(8,128)}), f32[8192,128]{1,0:T(8,128)}) %all-gather.14.cloned.1.call-update) | async-done | bytes 4194320 | tf_op jit(solution)/shard_map/all_gather | solution.py:25
  349.3 4.6 rev.9
  353.9 109.8 %while.33 = (s32[]{:T(128)}, f32[256,128]{1,0:T(8,128)S(1)}, f32[256]{0:T(256)S(1)}, s32[]{:T(128)}, f32[32,256,128]{2,1,0:T(8,128)}, /*index=5*/f32[32,1]{0,1:T(1,128)S(1)}, f32[32,256]{1,0:T(8,128)}, s32[]{:T(128)}, s32[]{:T(128)}) while((s32[]{:T(128)}, f32[256,128]{1,0:T(8,128)S(1)}, f32[256]{0:T(256)S(1)}, s32[]{:T(128)}, ...), condition=%wide.region_21.22_spmd.clone, body=%wide.region_20.21_spmd.clone.sunk | while | flops 132101 | bytes 398487 | solution.py:37
  354.5 1.6 fusion.108
  358.0 1.6 fusion.108
  361.5 1.6 fusion.108
  368.6 1.6 fusion.108
  372.2 1.6 fusion.108
  375.7 1.6 fusion.108
  379.3 1.6 fusion.108
  386.3 1.6 fusion.108
  469.7 139.8 %all-reduce.4.cloned.1.call-done = (f32[8,128,128]{1,2,0:T(8,128)}, f32[1,128,128]{1,2,0:T(8,128)}) async-done(((f32[8,128,128]{1,2,0:T(8,128)}, f32[1,128,128]{1,2,0:T(8,128)}), (f32[8,128,128]{1,2,0:T(8,128)}, f32[1,128,128]{1,2,0:T(8,128)})) %all-reduce.4.cloned.1.call-update) | async-done | bytes 589840 | tf_op jit(solution)/shard_map/psum | solution.py:182
  609.5 1.8 multiply_reduce_fusion
  614.0 1.8 fusion.43
  615.8 17.6 %psum.23 = f32[]{:T(128)} all-reduce(f32[]{:T(128)S(6)} %add.151), channel_id=1, replica_groups=mesh['seq'=32,'head'=8] {'head'}, use_global_device_ids=true, to_apply=%region_28.29 | all-reduce | flops 1 | bytes 8 | tf_op jit(solution)/shard_map/psum | solution.py:183
  (273 shorter events, 162.3 us)
Async XLA Ops:
  7.2 133.1 %copy-start = (f32[8,128,128]{2,1,0:T(8,128)S(1)}, f32[8,128,128]{2,1,0:T(8,128)}, u32[]{:S(2)}) copy-start(f32[8,128,128]{2,1,0:T(8,128)} %param.16) | copy-start | bytes 1572868
  7.2 138.4 %all-gather.10.cloned.1.call-start = ((), (), s32[]{:S(2)}) async-start(), calls=%async_computation.1 | async-start | bytes 1081344 | tf_op jit(solution)/shard_map/all_gather | solution.py:89
  7.9 164.8 %all-gather.12.cloned.1.call-start = ((), (), s32[]{:S(2)}) async-start(), calls=%async_computation.2 | async-start | bytes 4325376 | tf_op jit(solution)/shard_map/all_gather | solution.py:25
  14.7 130.9 %all-to-all-start = ((bf16[32,128,128]{2,1,0:T(8,128)(2,1)}), bf16[32,128,128]{2,1,0:T(8,128)(2,1)}, u32[]{:S(2)}, u32[]{:S(2)}) async-start(bf16[32,128,128]{2,1,0:T(8,128)(2,1)} %stack.2), calls=%async_computation | async-start | bytes 2097152 | tf_op jit(solution)/shard_map/all_to_all | solution.py:16
  26.7 322.6 %all-gather.14.cloned.1.call-start = ((), (), s32[]{:S(2)}) async-start(), calls=%async_computation.3 | async-start | bytes 4325376 | tf_op jit(solution)/shard_map/all_gather | solution.py:25
  145.6 155.2 %copy-start.1 = (bf16[128,128]{1,0:T(8,128)(2,1)S(1)}, bf16[128,128]{1,0:T(8,128)(2,1)}, u32[]{:S(2)}) copy-start(bf16[128,128]{1,0:T(8,128)(2,1)} %param.14) | copy-start | bytes 98308
  267.3 342.2 %all-reduce.4.cloned.1.call-start = ((), (), s32[]{:S(2)}) async-start(), calls=%async_computation.4 | async-start | bytes 1179648 | tf_op jit(solution)/shard_map/psum | solution.py:182
Sparse Core Ops, SparseCore 0:
  10.6 78.2 all-gather.9
  91.5 81.1 all-gather.11
  267.4 81.8 all-gather.13
  466.6 142.8 all-reduce.3
